TPU v7x, 256 devices: a whole 4x4x8 slice. The times are simulated.
256 devices in a mesh: tm: 8 (over z), tile: 32 (over y, x, core).
Axes of the slice: x: 4, y: 4, z: 8, core: 2. Of those that a mesh axis runs over, the one named last changes fastest.
Arguments:
- heads: float32 [8, 3, 512, 4096], P('tm', None, 'tile'), may hold values from -6 to 6
- capacity: float32 [512, 4096], P('tile'), may hold values from 0.5 to 2
- cond_row: float32 [512, 4096], P('tile'), may hold values from 0.1 to 1
- cond_col: float32 [512, 4096], P('tile'), may hold values from 0.1 to 1
- terminal: float32 [2, 512, 4096], P(None, 'tile'), may hold values from -6 to 6
- obs_cell: int32 [8, 2, 512], P('tm'), may hold values from 0 to 2097151
- obs_weight: float32 [8, 2, 2, 512], P('tm'), may hold values from -8 to 8
- block_mask: int32 [4, 32], replicated, may hold values 0 or 1
Outputs:
- adjoint_start: float32 [8, 2, 512, 4096], P('tm', None, 'tile')
- cond_sens: float32 [512, 4096], P('tile', 'tm')
- storage_sens: float32 [2], replicated
Inputs may be any that keep to these rules, and one draw needn't show every extreme that they name: `obs_cell`: row * 4096 + column of an observed cell; a cell may repeat.
All inputs are finite; a program needn't handle non-finite values.
Results may differ from a plain program's by a relative error of at most 0.0003.
Values sent between devices are 32-bit elements; how exact they have to be, the bound alone decides.
A program may use at most 64 MiB of HBM per device.

v0:
```python
import jax
import jax.numpy as jnp
from jax import lax
from jax.sharding import Mesh
from jax.sharding import PartitionSpec as P

BLOCK = 128
STEPS = 2
SWEEPS = 2
TILE = ("tile_0", "tile_1", "tile_2")
TM_TILE = ("tm", "tile_0", "tile_1", "tile_2")


def shifted(value, axis, steps):
    count = lax.axis_size(axis)
    leading, last = (max(0, -steps), min(count, count - steps))
    return lax.ppermute(value, axis, [(source, source + steps) for source in range(leading, last)])


def with_halo(value, sides, width):
    for axis, dim in sides:
        size, length = (lax.axis_size(axis), value.shape[dim])
        up = [(i, (i + 1) % size) for i in range(size - 1)]
        down = [(j, i) for i, j in up]
        last = lax.slice_in_dim(value, length - width, length, axis=dim)
        leading = lax.slice_in_dim(value, 0, width, axis=dim)
        before = lax.ppermute(last, axis, up)
        after = lax.ppermute(leading, axis, down)
        value = jnp.concatenate([before, value, after], axis=dim)
    return value


def one_axis_at_a_time(value, axes):
    for axis in axes:
        value = lax.psum(value, axis)
    return value


def shards(heads, capacity, cond_row, cond_col, terminal, obs_cell, obs_weight, block_mask):
    rows_here = capacity.shape[0]
    width = capacity.shape[1]
    members = terminal.shape[0]
    tile_index = lax.axis_index(TILE)
    section = lax.axis_index("tm")
    sections = lax.axis_size("tm")
    global_rows = tile_index * rows_here + jnp.arange(rows_here + 1, dtype=jnp.int32)
    block_rows = block_mask.shape[0]
    picker = (
        global_rows[:, None] // BLOCK == jnp.arange(block_rows, dtype=jnp.int32)[None, :]
    ).astype(jnp.float32)
    coarse = jnp.dot(picker, block_mask.astype(jnp.float32), precision=lax.Precision.HIGHEST)
    active_all = jnp.repeat(coarse, BLOCK, axis=1)
    active = active_all[:-1]
    next_active = active_all[1:]
    zero_col = jnp.zeros((rows_here, 1), jnp.float32)
    pair = active * jnp.concatenate([active[:, 1:], zero_col], axis=1)
    east = cond_row * pair
    west = jnp.concatenate([zero_col, east[:, :-1]], axis=1)
    south = cond_col * active * next_active
    upper_rim = shifted(south[-1:], TILE, 1)
    north = jnp.concatenate([upper_rim, south[:-1]], axis=0)
    diagonal = capacity + east + west + south + north
    coeff_stack = jnp.stack([east, west, south, north, diagonal])
    coeff_wide = with_halo(coeff_stack, ((TILE, 1),), SWEEPS - 1)
    east_wide = coeff_wide[0]
    west_wide = coeff_wide[1]
    south_wide = coeff_wide[2]
    north_wide = coeff_wide[3]
    diag_wide = jnp.where(coeff_wide[4] > 0.0, coeff_wide[4], 1.0)
    cell_row = obs_cell[0] // width
    cell_col = obs_cell[0] % width
    local_row = cell_row - tile_index * rows_here
    inside = (local_row >= 0) & (local_row < rows_here)
    local_row = jnp.where(inside, local_row, rows_here)
    row_range = jnp.arange(rows_here, dtype=jnp.int32)
    col_range = jnp.arange(width, dtype=jnp.int32)
    per_group = members // members
    rounds = sections + members - 1
    zero_cols = jnp.zeros((per_group, rows_here, 1), jnp.float32)

    def forcing(step, first):
        weights = lax.dynamic_slice_in_dim(obs_weight[0, step], first, per_group, 0)
        row_hit = (local_row[step][None, :] == row_range[:, None]).astype(jnp.float32)
        col_hit = (cell_col[step][:, None] == col_range[None, :]).astype(jnp.float32)
        weighted_rows = weights[:, None, :] * row_hit[None, :, :]
        return jnp.einsum("gro,oc->grc", weighted_rows, col_hit, precision=lax.Precision.HIGHEST)

    def slab_sweeps(field, rhs):
        joined = jnp.concatenate([field, rhs], axis=0)
        wide = with_halo(joined, ((TILE, 1),), SWEEPS)
        current = wide[:per_group]
        rhs_wide = wide[per_group:]
        for sweep_index in range(SWEEPS):
            count = current.shape[1] - 2
            above = current[:, :-2]
            below = current[:, 2:]
            middle = current[:, 1:-1]
            edge = jnp.zeros((per_group, count, 1), jnp.float32)
            left = jnp.concatenate([edge, middle[:, :, :-1]], axis=2)
            right = jnp.concatenate([middle[:, :, 1:], edge], axis=2)
            rhs_part = rhs_wide[:, sweep_index + 1 : sweep_index + 1 + count]
            east_part = east_wide[sweep_index : sweep_index + count]
            west_part = west_wide[sweep_index : sweep_index + count]
            south_part = south_wide[sweep_index : sweep_index + count]
            north_part = north_wide[sweep_index : sweep_index + count]
            diag_part = diag_wide[sweep_index : sweep_index + count]
            current = (
                rhs_part
                + east_part * right
                + west_part * left
                + south_part * below
                + north_part * above
            ) / diag_part
        return current

    def one_round(turn, carry):
        incoming, adjoint_out, sens_local, storage_part = carry
        group = turn - (sections - 1 - section)
        valid = (group >= 0) & (group < members)
        first = jnp.clip(group, 0, members - 1) * per_group
        ending = lax.dynamic_slice_in_dim(terminal, first, per_group, 0)
        field = jnp.where(section == sections - 1, ending, incoming)
        sens_add = jnp.zeros((rows_here, width), jnp.float32)
        store_add = jnp.zeros((per_group,), jnp.float32)
        for step in reversed(range(STEPS)):
            rhs = active * (capacity * field + forcing(step, first))
            field = slab_sweeps(field, rhs)
            later = heads[0, step + 1]
            earlier = heads[0, step]
            head_step = jnp.concatenate([later[:, 1:] - later[:, :-1], zero_col], axis=1)
            adj_step = jnp.concatenate([field[:, :, 1:] - field[:, :, :-1], zero_cols], axis=2)
            sens_add = sens_add + jnp.sum(adj_step * head_step * pair, axis=0)
            store_add = store_add + jnp.sum(field * capacity * (later - earlier), axis=(1, 2))
        sens_local = sens_local + jnp.where(valid, sens_add, 0.0)
        old_store = lax.dynamic_slice_in_dim(storage_part, first, per_group, 0)
        storage_part = lax.dynamic_update_slice_in_dim(
            storage_part, jnp.where(valid, old_store + store_add, old_store), first, 0
        )
        old_field = lax.dynamic_slice_in_dim(adjoint_out, first, per_group, 0)
        adjoint_out = lax.dynamic_update_slice_in_dim(
            adjoint_out, jnp.where(valid, field, old_field), first, 0
        )
        incoming = shifted(field, "tm", -1)
        return (incoming, adjoint_out, sens_local, storage_part)

    start = (
        jnp.zeros((per_group, rows_here, width), jnp.float32),
        jnp.zeros((members, rows_here, width), jnp.float32),
        jnp.zeros((rows_here, width), jnp.float32),
        jnp.zeros((members,), jnp.float32),
    )
    incoming, adjoint_out, sens_local, storage_part = lax.fori_loop(0, rounds, one_round, start)
    storage = one_axis_at_a_time(storage_part, TM_TILE)
    sens = lax.psum_scatter(sens_local, "tm", scatter_dimension=1, tiled=True)
    return (adjoint_out[None], sens, storage)


def solution(mesh):
    torus = Mesh(
        mesh.devices.reshape(mesh.shape["tm"], 4, 4, 2), ("tm", "tile_0", "tile_1", "tile_2")
    )
    in_specs = (
        P("tm", None, TILE, None),
        P(TILE, None),
        P(TILE, None),
        P(TILE, None),
        P(None, TILE, None),
        P("tm", None, None),
        P("tm", None, None, None),
        P(),
    )
    out_specs = (P("tm", None, TILE, None), P(TILE, "tm"), P())
    return jax.shard_map(
        shards, mesh=torus, in_specs=in_specs, out_specs=out_specs, check_vma=False
    )
```

profile of v0, /device:TPU:1, one launch (start us, length us, event | category | flops | bytes accessed | tf_op | source)
XLA Modules:
  0.0 500.7 jit_solution(12982076027055706300)
XLA Ops:
  10.1 4.5 collective-permute-start.5
  29.5 415.2 %while.23 = (s32[]{:T(128)}, f32[1,16,4096]{2,1,0:T(8,128)}, f32[2,16,4096]{2,1,0:T(8,128)}, f32[16,4096]{1,0:T(8,128)}, f32[2]{0:T(128)}, /*index=5*/f32[16,409...) while((s32[]{:T(128)}, f32[1,16,4096]{2,1,0:T(8,128)}, ...), condition=%wide.region_3.4_spmd.clone.clone, body=%wide.region_0.3_spmd.clone.clone.sunk | while | flops 815185920 | bytes 47845776 | solution.py:152
  84.8 5.2 %collective-permute-done.1 = f32[2,2,4096]{2,1,0:T(2,128)} collective-permute-done((f32[2,2,4096]{2,1,0:T(2,128)}, f32[2,2,4096]{2,1,0:T(2,128)}, u32[]{:S(2)}, u32[]{:S(2)}) %collective-permute-start.1) | collective-permute-done | bytes 65568 | tf_op jit(solution)/shard_map/while/body/eval_jaxpr/ppermute | solution.py:28
  100.7 5.1 %collective-permute-done.3 = f32[2,2,4096]{2,1,0:T(2,128)S(1)} collective-permute-done((f32[2,2,4096]{2,1,0:T(2,128)S(1)}, f32[2,2,4096]{2,1,0:T(2,128)S(1)}, u32[]{:S(2)}, u32[]{:S(2)}) %collective-permute-start.3) | collective-permute-done | bytes 65568 | tf_op jit(solution)/shard_map/while/body/eval_jaxpr/ppermute | solution.py:28
  130.0 4.9 collective-permute-done.1
  145.7 6.0 %collective-permute-done.3 = f32[2,2,4096]{2,1,0:T(2,128)S(1)} collective-permute-done((f32[2,2,4096]{2,1,0:T(2,128)S(1)}, f32[2,2,4096]{2,1,0:T(2,128)S(1)}, u32[]{:S(2)}, u32[]{:S(2)}) %collective-permute-start.3) | collective-permute-done | bytes 65568 | tf_op jit(solution)/shard_map/while/body/eval_jaxpr/ppermute | solution.py:28
  175.8 4.9 collective-permute-done.1
  191.5 6.0 %collective-permute-done.3 = f32[2,2,4096]{2,1,0:T(2,128)S(1)} collective-permute-done((f32[2,2,4096]{2,1,0:T(2,128)S(1)}, f32[2,2,4096]{2,1,0:T(2,128)S(1)}, u32[]{:S(2)}, u32[]{:S(2)}) %collective-permute-start.3) | collective-permute-done | bytes 65568 | tf_op jit(solution)/shard_map/while/body/eval_jaxpr/ppermute | solution.py:28
  222.8 4.9 collective-permute-done.1
  238.5 5.9 %collective-permute-done.3 = f32[2,2,4096]{2,1,0:T(2,128)S(1)} collective-permute-done((f32[2,2,4096]{2,1,0:T(2,128)S(1)}, f32[2,2,4096]{2,1,0:T(2,128)S(1)}, u32[]{:S(2)}, u32[]{:S(2)}) %collective-permute-start.3) | collective-permute-done | bytes 65568 | tf_op jit(solution)/shard_map/while/body/eval_jaxpr/ppermute | solution.py:28
  251.6 4.0 collective-permute-done.4
  269.8 4.9 collective-permute-done.1
  285.5 5.9 %collective-permute-done.3 = f32[2,2,4096]{2,1,0:T(2,128)S(1)} collective-permute-done((f32[2,2,4096]{2,1,0:T(2,128)S(1)}, f32[2,2,4096]{2,1,0:T(2,128)S(1)}, u32[]{:S(2)}, u32[]{:S(2)}) %collective-permute-start.3) | collective-permute-done | bytes 65568 | tf_op jit(solution)/shard_map/while/body/eval_jaxpr/ppermute | solution.py:28
  298.7 4.0 collective-permute-done.4
  316.9 4.9 collective-permute-done.1
  332.6 5.9 %collective-permute-done.3 = f32[2,2,4096]{2,1,0:T(2,128)S(1)} collective-permute-done((f32[2,2,4096]{2,1,0:T(2,128)S(1)}, f32[2,2,4096]{2,1,0:T(2,128)S(1)}, u32[]{:S(2)}, u32[]{:S(2)}) %collective-permute-start.3) | collective-permute-done | bytes 65568 | tf_op jit(solution)/shard_map/while/body/eval_jaxpr/ppermute | solution.py:28
  363.9 4.9 collective-permute-done.1
  379.7 5.9 %collective-permute-done.3 = f32[2,2,4096]{2,1,0:T(2,128)S(1)} collective-permute-done((f32[2,2,4096]{2,1,0:T(2,128)S(1)}, f32[2,2,4096]{2,1,0:T(2,128)S(1)}, u32[]{:S(2)}, u32[]{:S(2)}) %collective-permute-start.3) | collective-permute-done | bytes 65568 | tf_op jit(solution)/shard_map/while/body/eval_jaxpr/ppermute | solution.py:28
  411.0 4.9 collective-permute-done.1
  426.7 5.9 %collective-permute-done.3 = f32[2,2,4096]{2,1,0:T(2,128)S(1)} collective-permute-done((f32[2,2,4096]{2,1,0:T(2,128)S(1)}, f32[2,2,4096]{2,1,0:T(2,128)S(1)}, u32[]{:S(2)}, u32[]{:S(2)}) %collective-permute-start.3) | collective-permute-done | bytes 65568 | tf_op jit(solution)/shard_map/while/body/eval_jaxpr/ppermute | solution.py:28
  444.6 16.4 %psum.28 = f32[2]{0:T(128)S(1)} all-reduce(f32[2]{0:T(128)} %get-tuple-element.583), channel_id=1, replica_groups=mesh['tm'=8,'tile_0'=4,'tile_1'=4,'tile_2'=2] {'tm'}, use_global_device_ids=true, to_apply=%region_5.6 | all-reduce | flops 2 | bytes 16 | tf_op jit(solution)/shard_map/psum | solution.py:35
  461.0 10.7 %psum.29 = f32[2]{0:T(128)S(1)} all-reduce(f32[2]{0:T(128)S(1)} %psum.28), channel_id=1, replica_groups=mesh['tm'=8,'tile_0'=4,'tile_1'=4,'tile_2'=2] {'tile_0'}, use_global_device_ids=true, to_apply=%region_6.7 | all-reduce | flops 2 | bytes 16 | tf_op jit(solution)/shard_map/psum | solution.py:35
  471.7 13.6 %psum.30 = f32[2]{0:T(128)S(1)} all-reduce(f32[2]{0:T(128)S(1)} %psum.29), channel_id=1, replica_groups=mesh['tm'=8,'tile_0'=4,'tile_1'=4,'tile_2'=2] {'tile_1'}, use_global_device_ids=true, to_apply=%region_7.8 | all-reduce | flops 2 | bytes 16 | tf_op jit(solution)/shard_map/psum | solution.py:35
  485.3 8.6 %psum.31 = f32[2]{0:T(128)} all-reduce(f32[2]{0:T(128)S(1)} %psum.30), channel_id=1, replica_groups=mesh['tm'=8,'tile_0'=4,'tile_1'=4,'tile_2'=2] {'tile_2'}, use_global_device_ids=true, to_apply=%region_8.9 | all-reduce | flops 2 | bytes 16 | tf_op jit(solution)/shard_map/psum | solution.py:35
  (654 shorter events, 323.3 us)
Async XLA Ops:
  7.2 486.7 %reduce-scatter.2.cloned.1.call-start = ((), (), s32[]{:S(2)}) async-start(), calls=%async_computation.1 | async-start | bytes 294912 | tf_op jit(solution)/shard_map/reduce_scatter | solution.py:154
  62.0 8.6 %collective-permute-start.4 = (f32[1,16,4096]{2,1,0:T(8,128)S(1)}, f32[1,16,4096]{2,1,0:T(8,128)S(1)}, u32[]{:S(2)}, u32[]{:S(2)}) collective-permute-start(f32[1,16,4096]{2,1,0:T(8,128)S(1)} %get-tuple-element.1044), channel_id=1, source_target_pairs={{32,0},{64,32},{96,64},{128,96},{160,128},{192,160},{224,192},{33,... | collective-permute-start | bytes 786440 | tf_op jit(solution)/shard_map/while/body/eval_jaxpr/ppermute | solution.py:17
  81.7 8.3 %collective-permute-start.1 = (f32[2,2,4096]{2,1,0:T(2,128)}, f32[2,2,4096]{2,1,0:T(2,128)}, u32[]{:S(2)}, u32[]{:S(2)}) collective-permute-start(f32[2,2,4096]{2,1,0:T(2,128)} %get-tuple-element.1030), channel_id=1, source_target_pairs={{1,0},{2,1},{3,2},{4,3},{5,4},{6,5},{7,6},{8,7},{9,8},{10,9},{11,1... | collective-permute-start | bytes 196616 | tf_op jit(solution)/shard_map/while/body/eval_jaxpr/ppermute | solution.py:28
  98.2 7.7 %collective-permute-start.3 = (f32[2,2,4096]{2,1,0:T(2,128)S(1)}, f32[2,2,4096]{2,1,0:T(2,128)S(1)}, u32[]{:S(2)}, u32[]{:S(2)}) collective-permute-start(f32[2,2,4096]{2,1,0:T(2,128)S(1)} %get-tuple-element.1039), channel_id=1, source_target_pairs={{1,0},{2,1},{3,2},{4,3},{5,4},{6,5},{7,6},{8,7},{9,8},{10,9},{11,1... | collective-permute-start | bytes 196616 | tf_op jit(solution)/shard_map/while/body/eval_jaxpr/ppermute | solution.py:28
  108.4 7.4 %collective-permute-start.4 = (f32[1,16,4096]{2,1,0:T(8,128)S(1)}, f32[1,16,4096]{2,1,0:T(8,128)S(1)}, u32[]{:S(2)}, u32[]{:S(2)}) collective-permute-start(f32[1,16,4096]{2,1,0:T(8,128)S(1)} %get-tuple-element.1044), channel_id=1, source_target_pairs={{32,0},{64,32},{96,64},{128,96},{160,128},{192,160},{224,192},{33,... | collective-permute-start | bytes 786440 | tf_op jit(solution)/shard_map/while/body/eval_jaxpr/ppermute | solution.py:17
  143.1 8.6 %collective-permute-start.3 = (f32[2,2,4096]{2,1,0:T(2,128)S(1)}, f32[2,2,4096]{2,1,0:T(2,128)S(1)}, u32[]{:S(2)}, u32[]{:S(2)}) collective-permute-start(f32[2,2,4096]{2,1,0:T(2,128)S(1)} %get-tuple-element.1039), channel_id=1, source_target_pairs={{1,0},{2,1},{3,2},{4,3},{5,4},{6,5},{7,6},{8,7},{9,8},{10,9},{11,1... | collective-permute-start | bytes 196616 | tf_op jit(solution)/shard_map/while/body/eval_jaxpr/ppermute | solution.py:28
  154.2 7.4 %collective-permute-start.4 = (f32[1,16,4096]{2,1,0:T(8,128)S(1)}, f32[1,16,4096]{2,1,0:T(8,128)S(1)}, u32[]{:S(2)}, u32[]{:S(2)}) collective-permute-start(f32[1,16,4096]{2,1,0:T(8,128)S(1)} %get-tuple-element.1044), channel_id=1, source_target_pairs={{32,0},{64,32},{96,64},{128,96},{160,128},{192,160},{224,192},{33,... | collective-permute-start | bytes 786440 | tf_op jit(solution)/shard_map/while/body/eval_jaxpr/ppermute | solution.py:17
  189.0 8.6 %collective-permute-start.3 = (f32[2,2,4096]{2,1,0:T(2,128)S(1)}, f32[2,2,4096]{2,1,0:T(2,128)S(1)}, u32[]{:S(2)}, u32[]{:S(2)}) collective-permute-start(f32[2,2,4096]{2,1,0:T(2,128)S(1)} %get-tuple-element.1039), channel_id=1, source_target_pairs={{1,0},{2,1},{3,2},{4,3},{5,4},{6,5},{7,6},{8,7},{9,8},{10,9},{11,1... | collective-permute-start | bytes 196616 | tf_op jit(solution)/shard_map/while/body/eval_jaxpr/ppermute | solution.py:28
  200.0 8.5 %collective-permute-start.4 = (f32[1,16,4096]{2,1,0:T(8,128)S(1)}, f32[1,16,4096]{2,1,0:T(8,128)S(1)}, u32[]{:S(2)}, u32[]{:S(2)}) collective-permute-start(f32[1,16,4096]{2,1,0:T(8,128)S(1)} %get-tuple-element.1044), channel_id=1, source_target_pairs={{32,0},{64,32},{96,64},{128,96},{160,128},{192,160},{224,192},{33,... | collective-permute-start | bytes 786440 | tf_op jit(solution)/shard_map/while/body/eval_jaxpr/ppermute | solution.py:17
  220.5 7.2 %collective-permute-start.1 = (f32[2,2,4096]{2,1,0:T(2,128)}, f32[2,2,4096]{2,1,0:T(2,128)}, u32[]{:S(2)}, u32[]{:S(2)}) collective-permute-start(f32[2,2,4096]{2,1,0:T(2,128)} %get-tuple-element.1030), channel_id=1, source_target_pairs={{1,0},{2,1},{3,2},{4,3},{5,4},{6,5},{7,6},{8,7},{9,8},{10,9},{11,1... | collective-permute-start | bytes 196616 | tf_op jit(solution)/shard_map/while/body/eval_jaxpr/ppermute | solution.py:28
  235.9 8.5 %collective-permute-start.3 = (f32[2,2,4096]{2,1,0:T(2,128)S(1)}, f32[2,2,4096]{2,1,0:T(2,128)S(1)}, u32[]{:S(2)}, u32[]{:S(2)}) collective-permute-start(f32[2,2,4096]{2,1,0:T(2,128)S(1)} %get-tuple-element.1039), channel_id=1, source_target_pairs={{1,0},{2,1},{3,2},{4,3},{5,4},{6,5},{7,6},{8,7},{9,8},{10,9},{11,1... | collective-permute-start | bytes 196616 | tf_op jit(solution)/shard_map/while/body/eval_jaxpr/ppermute | solution.py:28
  246.9 8.7 %collective-permute-start.4 = (f32[1,16,4096]{2,1,0:T(8,128)S(1)}, f32[1,16,4096]{2,1,0:T(8,128)S(1)}, u32[]{:S(2)}, u32[]{:S(2)}) collective-permute-start(f32[1,16,4096]{2,1,0:T(8,128)S(1)} %get-tuple-element.1044), channel_id=1, source_target_pairs={{32,0},{64,32},{96,64},{128,96},{160,128},{192,160},{224,192},{33,... | collective-permute-start | bytes 786440 | tf_op jit(solution)/shard_map/while/body/eval_jaxpr/ppermute | solution.py:17
  267.6 7.2 %collective-permute-start.1 = (f32[2,2,4096]{2,1,0:T(2,128)}, f32[2,2,4096]{2,1,0:T(2,128)}, u32[]{:S(2)}, u32[]{:S(2)}) collective-permute-start(f32[2,2,4096]{2,1,0:T(2,128)} %get-tuple-element.1030), channel_id=1, source_target_pairs={{1,0},{2,1},{3,2},{4,3},{5,4},{6,5},{7,6},{8,7},{9,8},{10,9},{11,1... | collective-permute-start | bytes 196616 | tf_op jit(solution)/shard_map/while/body/eval_jaxpr/ppermute | solution.py:28
  283.0 8.5 %collective-permute-start.3 = (f32[2,2,4096]{2,1,0:T(2,128)S(1)}, f32[2,2,4096]{2,1,0:T(2,128)S(1)}, u32[]{:S(2)}, u32[]{:S(2)}) collective-permute-start(f32[2,2,4096]{2,1,0:T(2,128)S(1)} %get-tuple-element.1039), channel_id=1, source_target_pairs={{1,0},{2,1},{3,2},{4,3},{5,4},{6,5},{7,6},{8,7},{9,8},{10,9},{11,1... | collective-permute-start | bytes 196616 | tf_op jit(solution)/shard_map/while/body/eval_jaxpr/ppermute | solution.py:28
  294.0 8.7 %collective-permute-start.4 = (f32[1,16,4096]{2,1,0:T(8,128)S(1)}, f32[1,16,4096]{2,1,0:T(8,128)S(1)}, u32[]{:S(2)}, u32[]{:S(2)}) collective-permute-start(f32[1,16,4096]{2,1,0:T(8,128)S(1)} %get-tuple-element.1044), channel_id=1, source_target_pairs={{32,0},{64,32},{96,64},{128,96},{160,128},{192,160},{224,192},{33,... | collective-permute-start | bytes 786440 | tf_op jit(solution)/shard_map/while/body/eval_jaxpr/ppermute | solution.py:17
  314.6 7.2 %collective-permute-start.1 = (f32[2,2,4096]{2,1,0:T(2,128)}, f32[2,2,4096]{2,1,0:T(2,128)}, u32[]{:S(2)}, u32[]{:S(2)}) collective-permute-start(f32[2,2,4096]{2,1,0:T(2,128)} %get-tuple-element.1030), channel_id=1, source_target_pairs={{1,0},{2,1},{3,2},{4,3},{5,4},{6,5},{7,6},{8,7},{9,8},{10,9},{11,1... | collective-permute-start | bytes 196616 | tf_op jit(solution)/shard_map/while/body/eval_jaxpr/ppermute | solution.py:28
  330.0 8.5 %collective-permute-start.3 = (f32[2,2,4096]{2,1,0:T(2,128)S(1)}, f32[2,2,4096]{2,1,0:T(2,128)S(1)}, u32[]{:S(2)}, u32[]{:S(2)}) collective-permute-start(f32[2,2,4096]{2,1,0:T(2,128)S(1)} %get-tuple-element.1039), channel_id=1, source_target_pairs={{1,0},{2,1},{3,2},{4,3},{5,4},{6,5},{7,6},{8,7},{9,8},{10,9},{11,1... | collective-permute-start | bytes 196616 | tf_op jit(solution)/shard_map/while/body/eval_jaxpr/ppermute | solution.py:28
  341.0 8.7 %collective-permute-start.4 = (f32[1,16,4096]{2,1,0:T(8,128)S(1)}, f32[1,16,4096]{2,1,0:T(8,128)S(1)}, u32[]{:S(2)}, u32[]{:S(2)}) collective-permute-start(f32[1,16,4096]{2,1,0:T(8,128)S(1)} %get-tuple-element.1044), channel_id=1, source_target_pairs={{32,0},{64,32},{96,64},{128,96},{160,128},{192,160},{224,192},{33,... | collective-permute-start | bytes 786440 | tf_op jit(solution)/shard_map/while/body/eval_jaxpr/ppermute | solution.py:17
  361.7 7.2 %collective-permute-start.1 = (f32[2,2,4096]{2,1,0:T(2,128)}, f32[2,2,4096]{2,1,0:T(2,128)}, u32[]{:S(2)}, u32[]{:S(2)}) collective-permute-start(f32[2,2,4096]{2,1,0:T(2,128)} %get-tuple-element.1030), channel_id=1, source_target_pairs={{1,0},{2,1},{3,2},{4,3},{5,4},{6,5},{7,6},{8,7},{9,8},{10,9},{11,1... | collective-permute-start | bytes 196616 | tf_op jit(solution)/shard_map/while/body/eval_jaxpr/ppermute | solution.py:28
  377.1 8.5 %collective-permute-start.3 = (f32[2,2,4096]{2,1,0:T(2,128)S(1)}, f32[2,2,4096]{2,1,0:T(2,128)S(1)}, u32[]{:S(2)}, u32[]{:S(2)}) collective-permute-start(f32[2,2,4096]{2,1,0:T(2,128)S(1)} %get-tuple-element.1039), channel_id=1, source_target_pairs={{1,0},{2,1},{3,2},{4,3},{5,4},{6,5},{7,6},{8,7},{9,8},{10,9},{11,1... | collective-permute-start | bytes 196616 | tf_op jit(solution)/shard_map/while/body/eval_jaxpr/ppermute | solution.py:28
  388.1 8.7 %collective-permute-start.4 = (f32[1,16,4096]{2,1,0:T(8,128)S(1)}, f32[1,16,4096]{2,1,0:T(8,128)S(1)}, u32[]{:S(2)}, u32[]{:S(2)}) collective-permute-start(f32[1,16,4096]{2,1,0:T(8,128)S(1)} %get-tuple-element.1044), channel_id=1, source_target_pairs={{32,0},{64,32},{96,64},{128,96},{160,128},{192,160},{224,192},{33,... | collective-permute-start | bytes 786440 | tf_op jit(solution)/shard_map/while/body/eval_jaxpr/ppermute | solution.py:17
  408.8 7.2 %collective-permute-start.1 = (f32[2,2,4096]{2,1,0:T(2,128)}, f32[2,2,4096]{2,1,0:T(2,128)}, u32[]{:S(2)}, u32[]{:S(2)}) collective-permute-start(f32[2,2,4096]{2,1,0:T(2,128)} %get-tuple-element.1030), channel_id=1, source_target_pairs={{1,0},{2,1},{3,2},{4,3},{5,4},{6,5},{7,6},{8,7},{9,8},{10,9},{11,1... | collective-permute-start | bytes 196616 | tf_op jit(solution)/shard_map/while/body/eval_jaxpr/ppermute | solution.py:28
  424.1 8.5 %collective-permute-start.3 = (f32[2,2,4096]{2,1,0:T(2,128)S(1)}, f32[2,2,4096]{2,1,0:T(2,128)S(1)}, u32[]{:S(2)}, u32[]{:S(2)}) collective-permute-start(f32[2,2,4096]{2,1,0:T(2,128)S(1)} %get-tuple-element.1039), channel_id=1, source_target_pairs={{1,0},{2,1},{3,2},{4,3},{5,4},{6,5},{7,6},{8,7},{9,8},{10,9},{11,1... | collective-permute-start | bytes 196616 | tf_op jit(solution)/shard_map/while/body/eval_jaxpr/ppermute | solution.py:28
  435.2 8.7 %collective-permute-start.4 = (f32[1,16,4096]{2,1,0:T(8,128)S(1)}, f32[1,16,4096]{2,1,0:T(8,128)S(1)}, u32[]{:S(2)}, u32[]{:S(2)}) collective-permute-start(f32[1,16,4096]{2,1,0:T(8,128)S(1)} %get-tuple-element.1044), channel_id=1, source_target_pairs={{32,0},{64,32},{96,64},{128,96},{160,128},{192,160},{224,192},{33,... | collective-permute-start | bytes 786440 | tf_op jit(solution)/shard_map/while/body/eval_jaxpr/ppermute | solution.py:17
  (183 other events, 401.4 us)
Sparse Core Ops, SparseCore 0:
  444.8 42.2 reduce-scatter.1
where the time goes:
time: 504 us; the launch traced here: 501 us
  waiting for transfers between devices  129 us (26%)
  starting transfers between devices  106 us (21%)
  local copies, waits for them, and re-layouts  67 us (13%)
  other arithmetic  61.4 us (12%)
  matrix products  59.5 us (12%)
  blocking collectives  49.2 us (10%)
  loops' own time  14.6 us (3%)
  between operations  14.2 us (3%)
    ppermute x19, waiting for transfers between devices, with_halo(): after = lax.ppermute(leading, axis, down)  95.9 us
    dot_general x18, matrix products, forcing(): jnp.einsum('gro,oc->grc', weighted_rows, col_hit, precision=lax.Precision...  58.6 us
    psum x4, blocking collectives, one_axis_at_a_time(): value = lax.psum(value, axis)  49.2 us
    ppermute x19, starting transfers between devices, with_halo(): after = lax.ppermute(leading, axis, down)  44.8 us
    ppermute x19, starting transfers between devices, with_halo(): before = lax.ppermute(last, axis, up)  43.5 us
    ppermute x10, waiting for transfers between devices, shifted(): lax.ppermute(value, axis, [(source, source + steps) for source in range(l...  33.2 us
    while x306, local copies, waits for them, and re-layouts  30.8 us
    ppermute x10, starting transfers between devices, shifted(): lax.ppermute(value, axis, [(source, source + steps) for source in range(l...  17.3 us
  transfers between devices with their start and end apart: 49, of which 28 were waited for; matrix products, arithmetic and copies ran while one was open for 2% of the time, Pallas kernels for 0%

commit v1 on v0

v1 whole, which is shorter than its diff:
```python
import functools

import jax
import jax.numpy as jnp
from jax import lax
from jax.experimental import pallas as pl
from jax.experimental.pallas import tpu as pltpu
from jax.sharding import PartitionSpec as P

STEPS = 2
LANES = 128
MESH = pl.DeviceIdType.MESH


def kernel(cfg, heads, cap, crow, ccol, term, ocell, oweight, mask, out_a, out_c, out_s,
           ext, field, mid, rhs, coef, force, cells, weights, head, saved, red_a, red_b, red_c,
           loc_sem, halo_send, halo_recv, obs_send, obs_recv, head_send, head_recv,
           mid_send, mid_recv, start_send, start_recv, red_send, red_recv):
    planes, tiles, inner, rows, cols, total_cols, block_rows, block_cols = cfg
    wide = cols + 2 * LANES
    tall = 3 * rows
    edge = cols + LANES
    total_rows = rows * tiles
    me = lax.axis_index("tm")
    tile = lax.axis_index("tile")
    above = lax.rem(tile + tiles - 1, tiles)
    below = lax.rem(tile + 1, tiles)
    group = tile // inner
    place = lax.rem(tile, inner)
    outer = tiles // inner

    def plane_at(d):
        return lax.rem(me + d, planes)

    def inner_at(d):
        return group * inner + lax.rem(place + d, inner)

    def outer_at(d):
        return lax.rem(group + d, outer) * inner + place

    def at(plane, row_tile):
        return {"tm": plane, "tile": row_tile}

    partners = [(plane_at(d), tile) for d in range(1, planes)]
    partners += [(me, above), (me, below)]
    partners += [(me, inner_at(d)) for d in range(1, inner)]
    partners += [(me, outer_at(d)) for d in range(1, outer)]
    barrier = pltpu.get_barrier_semaphore()
    for plane, row_tile in partners:
        pl.semaphore_signal(barrier, inc=1, device_id=at(plane, row_tile), device_id_type=MESH)

    def lane(offset):
        return pl.multiple_of(lax.rem(offset + total_cols, total_cols), LANES)

    first = me * cols
    pieces = [
        (lane(first - LANES), LANES, 0),
        (lane(first), cols, LANES),
        (lane(first + cols), LANES, LANES + cols),
    ]

    def own_parts(row):
        parts = []
        for start, size, to in pieces:
            for i, ref in enumerate((cap, crow, ccol)):
                parts.append((ref.at[:, pl.ds(start, size)],
                              ext.at[i, pl.ds(row, rows), pl.ds(to, size)]))
            parts.append((term.at[:, :, pl.ds(start, size)],
                          field.at[0, :, pl.ds(row, rows), pl.ds(to, size)]))
        return parts

    def head_parts(target, source):
        begin = lane(target * cols)
        after = lane(target * cols + cols)
        return [
            (heads.at[0, :, :, pl.ds(begin, cols)], head.at[source, :, :, pl.ds(0, cols)]),
            (heads.at[0, pl.ds(1, 2), :, pl.ds(after, LANES)],
             head.at[source, pl.ds(1, 2), :, pl.ds(cols, LANES)]),
        ]

    def obs_parts(source):
        return [(ocell.at[0], cells.at[source]), (oweight.at[0], weights.at[source])]

    local = []
    for src, dst in own_parts(rows) + head_parts(me, me) + obs_parts(me):
        copy = pltpu.make_async_copy(src, dst, loc_sem.at[len(local)])
        copy.start()
        local.append(copy)
    pl.semaphore_wait(barrier, len(partners))

    def remote(src, dst, send, recv, plane, row_tile):
        return pltpu.make_async_remote_copy(
            src_ref=src, dst_ref=dst, send_sem=send, recv_sem=recv,
            device_id=at(plane, row_tile), device_id_type=MESH)

    def obs_copies(d, source):
        return [remote(src, dst, obs_send.at[d, i], obs_recv.at[d, i], plane_at(d), tile)
                for i, (src, dst) in enumerate(obs_parts(source))]

    def head_copies(d, source):
        return [remote(src, dst, head_send.at[d, i], head_recv.at[d, i], plane_at(d), tile)
                for i, (src, dst) in enumerate(head_parts(plane_at(d), source))]

    sent = []
    for d in range(1, planes):
        sent += obs_copies(d, me)
    halos = []
    for way, (row, target) in enumerate(((2 * rows, above), (0, below))):
        for i, (src, dst) in enumerate(own_parts(row)):
            halos.append(remote(src, dst, halo_send.at[way, i], halo_recv.at[way, i], me, target))
    order = sorted(range(1, planes), key=lambda d: -min(d, planes - d))
    for copy in sent + halos:
        copy.start()
    sent_heads = []
    for d in order:
        sent_heads += head_copies(d, me)
    for copy in sent_heads:
        copy.start()

    for copy in local:
        copy.wait()
    for d in range(1, planes):
        for copy in obs_copies(d, plane_at(planes - d)):
            copy.wait_recv()

    row_ids = lax.broadcasted_iota(jnp.int32, (tall, 1), 0)
    col_ids = lax.broadcasted_iota(jnp.int32, (wide, 1), 0)

    def forcing(section, carry):
        for step in range(STEPS):
            cell = cells[section, step : step + 1, :]
            cell_row = cell // total_cols
            cell_col = cell - cell_row * total_cols
            near_row = lax.rem(cell_row - tile * rows + rows + total_rows, total_rows)
            near_col = lax.rem(cell_col - me * cols + LANES + total_cols, total_cols)
            row_hit = near_row == row_ids
            col_hit = jnp.where(near_col == col_ids, 1.0, 0.0).astype(jnp.bfloat16)
            parts = []
            for member in range(2):
                rest = weights[section, step, member : member + 1, :]
                for _ in range(3):
                    part = rest.astype(jnp.bfloat16).astype(jnp.float32)
                    rest = rest - part
                    parts.append(jnp.where(row_hit, part, 0.0).astype(jnp.bfloat16))
            stacked = jnp.concatenate(parts, axis=0)
            got = lax.dot_general(stacked, col_hit, (((1,), (1,)), ((), ())),
                                  preferred_element_type=jnp.float32)
            for member in range(2):
                begin = 3 * member * tall
                force[section, step, member] = (
                    got[begin : begin + tall]
                    + got[begin + tall : begin + 2 * tall]
                    + got[begin + 2 * tall : begin + 3 * tall])
        return carry

    lax.fori_loop(0, planes, forcing, 0)

    for copy in halos:
        copy.wait_recv()

    def activity(shift, j):
        row_tile = lax.rem(tile + shift + tiles, tiles)
        block = lax.rem(first - LANES + j * LANES + total_cols, total_cols) // block_cols
        return mask[(row_tile * rows) // block_rows, block].astype(jnp.float32)

    lane_id = lax.broadcasted_iota(jnp.int32, (rows, LANES), 1)
    row_id = lax.broadcasted_iota(jnp.int32, (rows, LANES), 0)
    act_bands, pair_bands, down_bands = [], [], []
    for band in range(3):
        act_row, pair_row, down_row = [], [], []
        last_row = lax.rem(tile + band - 1 + tiles, tiles) == tiles - 1
        for j in range(wide // LANES):
            here = activity(band - 1, j)
            last_col = lax.rem(first + j * LANES + total_cols, total_cols) == 0
            beside = jnp.where(last_col, 0.0, activity(band - 1, j + 1))
            under = jnp.where(last_row, 0.0, activity(band, j))
            act_row.append(jnp.full((rows, LANES), here, jnp.float32))
            pair_row.append(here * jnp.where(lane_id == LANES - 1, beside, here))
            down_row.append(here * jnp.where(row_id == rows - 1, under, here))
        act_bands.append(jnp.concatenate(act_row, axis=1))
        pair_bands.append(jnp.concatenate(pair_row, axis=1))
        down_bands.append(jnp.concatenate(down_row, axis=1))
    pair_core = pair_bands[1][:, LANES : LANES + cols]
    active = jnp.concatenate(act_bands, axis=0)
    east = ext[1] * jnp.concatenate(pair_bands, axis=0)
    south = ext[2] * jnp.concatenate(down_bands, axis=0)
    west = pltpu.roll(east, 1, 1)
    north = pltpu.roll(south, 1, 0)
    capacity = ext[0]
    inverse = 1.0 / (capacity + east + west + south + north)
    coef[0] = east * inverse
    coef[1] = west * inverse
    coef[2] = south * inverse
    coef[3] = north * inverse
    coef[4] = active * capacity * inverse
    coef[5] = active * inverse

    sub_id = lax.broadcasted_iota(jnp.int32, (1, 8, wide), 1)
    strips = tall // 8

    def stencil(source, i):
        start = pl.multiple_of(i * 8, 8)
        before = pl.multiple_of(jnp.maximum(i - 1, 0) * 8, 8)
        after = pl.multiple_of(jnp.minimum(i + 1, strips - 1) * 8, 8)
        here = source[:, pl.ds(start, 8), :]
        up = jnp.where(sub_id == 0, pltpu.roll(source[:, pl.ds(before, 8), :], 1, 1),
                       pltpu.roll(here, 1, 1))
        down = jnp.where(sub_id == 7, pltpu.roll(source[:, pl.ds(after, 8), :], 7, 1),
                         pltpu.roll(here, 7, 1))
        right = pltpu.roll(here, wide - 1, 2)
        left = pltpu.roll(here, 1, 2)
        strip = pl.ds(start, 8)
        total = (coef[0, strip, :][None] * right + coef[1, strip, :][None] * left
                 + coef[2, strip, :][None] * down + coef[3, strip, :][None] * up)
        return here, total, strip

    def one_step(now, section, step):
        def first_sweep(i, carry):
            here, total, strip = stencil(now, i)
            part = (coef[4, strip, :][None] * here
                    + coef[5, strip, :][None] * force[section, step, :, strip, :])
            rhs[:, strip, :] = part
            mid[:, strip, :] = part + total
            return carry

        def second_sweep(i, carry):
            _, total, strip = stencil(mid, i)
            now[:, strip, :] = rhs[:, strip, :] + total
            return carry

        lax.fori_loop(0, strips, first_sweep, 0)
        lax.fori_loop(0, strips, second_sweep, 0)
        saved[section, step] = now[:, rows : 2 * rows, LANES:]

    def start_copy(section, d):
        return remote(saved.at[section, 0, :, :, pl.ds(0, cols)],
                      out_a.at[0, :, :, pl.ds(pl.multiple_of(first, LANES), cols)],
                      start_send.at[d], start_recv.at[d], section, tile)

    def own_start():
        return pltpu.make_async_copy(
            saved.at[me, 0, :, :, pl.ds(0, cols)],
            out_a.at[0, :, :, pl.ds(pl.multiple_of(first, LANES), cols)],
            loc_sem.at[0])

    half = planes // 2
    mids = []
    for phase in range(2):
        now = field.at[phase]

        def one_section(turn, carry):
            section = planes - 1 - phase * half - turn
            for step in reversed(range(STEPS)):
                one_step(now, section, step)
            d = lax.rem(section - me + planes, planes)

            @pl.when(section != me)
            def _():
                start_copy(section, d).start()

            @pl.when(section == me)
            def _():
                own_start().start()

            return carry

        lax.fori_loop(0, half, one_section, 0)
        if phase == 0:
            core = pl.ds(rows, rows)
            field[1, :, rows : 2 * rows, :] = field[0, :, rows : 2 * rows, :]
            for way, (row, target) in enumerate(((2 * rows, above), (0, below))):
                copy = remote(field.at[0, :, core, :], field.at[1, :, pl.ds(row, rows), :],
                              mid_send.at[way], mid_recv.at[way], me, target)
                copy.start()
                mids.append(copy)
            for copy in mids:
                copy.wait_recv()

    for d in range(1, planes):
        for copy in head_copies(d, plane_at(planes - d)):
            copy.wait_recv()

    def sums(section, carry):
        sens, store_0, store_1 = carry
        for step in range(STEPS):
            a_0 = saved[section, step, 0]
            a_1 = saved[section, step, 1]
            later = head[section, step + 1]
            both = a_0 + a_1
            jump = ((pltpu.roll(both, edge - 1, 1) - both)
                    * (pltpu.roll(later, edge - 1, 1) - later))
            sens = sens + jump[:, :cols]
            change = later[:, :cols] - head[section, step, :, pl.ds(0, cols)]
            store_0 = store_0 + a_0[:, :cols] * change
            store_1 = store_1 + a_1[:, :cols] * change
        return sens, store_0, store_1

    zero = jnp.zeros((rows, cols), jnp.float32)
    sens, store_0, store_1 = lax.fori_loop(0, planes, sums, (zero, zero, zero))
    out_c[...] = sens * pair_core
    cap_core = ext[0, rows : 2 * rows, LANES : LANES + cols]
    tile_lane = lax.broadcasted_iota(jnp.int32, (8, LANES), 1)
    part = jnp.where(tile_lane == 0, jnp.sum(store_0 * cap_core), 0.0)
    part = jnp.where(tile_lane == 1, jnp.sum(store_1 * cap_core), part)

    reduce_sends = []

    def exchange(value, slots, place_here, count, partner, base):
        slots[place_here] = value
        copies = []
        for d in range(1, count):
            plane, row_tile = partner(d)
            copies.append(remote(slots.at[place_here], slots.at[place_here],
                                 red_send.at[base + d], red_recv.at[base + d], plane, row_tile))
        for copy in copies:
            copy.start()
        for d in range(1, count):
            source = lax.rem(place_here + count - d, count)
            plane, row_tile = partner(d)
            remote(slots.at[source], slots.at[source], red_send.at[base + d],
                   red_recv.at[base + d], plane, row_tile).wait_recv()
        reduce_sends.extend(copies)
        total = slots[0]
        for i in range(1, count):
            total = total + slots[i]
        return total

    part = exchange(part, red_b, place, inner, lambda d: (me, inner_at(d)), 0)
    part = exchange(part, red_c, group, outer, lambda d: (me, outer_at(d)), inner)
    part = exchange(part, red_a, me, planes, lambda d: (plane_at(d), tile), inner + outer)
    out_s[0] = jnp.sum(jnp.where(tile_lane[:1] == 0, part[:1], 0.0))
    out_s[1] = jnp.sum(jnp.where(tile_lane[:1] == 1, part[:1], 0.0))

    own_start().wait()
    for d in range(1, planes):
        source = plane_at(planes - d)
        remote(saved.at[me, 0, :, :, pl.ds(0, cols)],
               out_a.at[0, :, :, pl.ds(pl.multiple_of(source * cols, LANES), cols)],
               start_send.at[d], start_recv.at[d], plane_at(d), tile).wait_recv()
    for d in range(1, planes):
        start_copy(plane_at(d), d).wait_send()
    for copy in sent + halos + sent_heads + mids + reduce_sends:
        copy.wait_send()


def solution(mesh):
    planes, tiles = mesh.shape["tm"], mesh.shape["tile"]
    inner = min(8, tiles // 2)
    outer = tiles // inner

    def shards(heads, capacity, cond_row, cond_col, terminal, obs_cell, obs_weight, block_mask):
        rows, total_cols = capacity.shape
        cols = total_cols // planes
        wide, tall, edge = cols + 2 * LANES, 3 * rows, cols + LANES
        observed = obs_cell.shape[2]
        block_rows = rows * tiles // block_mask.shape[0]
        block_cols = total_cols // block_mask.shape[1]
        cfg = (planes, tiles, inner, rows, cols, total_cols, block_rows, block_cols)
        f32 = jnp.float32
        dma = pltpu.SemaphoreType.DMA
        any_spec = pl.BlockSpec(memory_space=pl.ANY)
        out = pl.pallas_call(
            functools.partial(kernel, cfg),
            out_shape=(
                jax.ShapeDtypeStruct((1, 2, rows, total_cols), f32),
                jax.ShapeDtypeStruct((rows, cols), f32),
                jax.ShapeDtypeStruct((2,), f32),
            ),
            in_specs=[any_spec] * 7 + [pl.BlockSpec(memory_space=pltpu.SMEM)],
            out_specs=(any_spec, pl.BlockSpec(memory_space=pltpu.VMEM),
                       pl.BlockSpec(memory_space=pltpu.SMEM)),
            scratch_shapes=[
                pltpu.VMEM((3, tall, wide), f32),
                pltpu.VMEM((2, 2, tall, wide), f32),
                pltpu.VMEM((2, tall, wide), f32),
                pltpu.VMEM((2, tall, wide), f32),
                pltpu.VMEM((6, tall, wide), f32),
                pltpu.VMEM((planes, STEPS, 2, tall, wide), f32),
                pltpu.VMEM((planes, STEPS, observed), jnp.int32),
                pltpu.VMEM((planes, STEPS, 2, observed), f32),
                pltpu.VMEM((planes, 3, rows, edge), f32),
                pltpu.VMEM((planes, STEPS, 2, rows, edge), f32),
                pltpu.VMEM((planes, 8, LANES), f32),
                pltpu.VMEM((inner, 8, LANES), f32),
                pltpu.VMEM((outer, 8, LANES), f32),
                dma((16,)),
                dma((2, 12)),
                dma((2, 12)),
                dma((planes, 2)),
                dma((planes, 2)),
                dma((planes, 2)),
                dma((planes, 2)),
                dma((2,)),
                dma((2,)),
                dma((planes,)),
                dma((planes,)),
                dma((planes + inner + outer,)),
                dma((planes + inner + outer,)),
            ],
            compiler_params=pltpu.CompilerParams(
                collective_id=0, has_side_effects=True, vmem_limit_bytes=48 * 1024 * 1024
            ),
        )(heads, capacity, cond_row, cond_col, terminal, obs_cell, obs_weight, block_mask)
        return out

    in_specs = (
        P("tm", None, "tile", None),
        P("tile", None),
        P("tile", None),
        P("tile", None),
        P(None, "tile", None),
        P("tm", None, None),
        P("tm", None, None, None),
        P(),
    )
    out_specs = (P("tm", None, "tile", None), P("tile", "tm"), P())
    return jax.shard_map(
        shards, mesh=mesh, in_specs=in_specs, out_specs=out_specs, check_vma=False
    )
```

time: 504 us -> 76.6 us (0.15)
  waiting for transfers between devices: 129 us -> 0 us
  starting transfers between devices: 106 us -> 0 us
  Pallas kernels: 0 us -> 66.5 us
  other arithmetic: 61.4 us -> 0 us
  matrix products: 59.5 us -> 0 us
  local copies, waits for them, and re-layouts: 67 us -> 9 us
  blocking collectives: 49.2 us -> 0 us
  loops' own time: 14.6 us -> 0 us
  between operations: 14.2 us -> 0.66 us
    ppermute x48 -> x0, waiting for transfers between devices: 129 us -> none  [the longest x19 95.9 us: with_halo(): after = lax.ppermute(leading, axis, down)]
    ppermute x48 -> x0, starting transfers between devices: 106 us -> none  [the longest x19 44.8 us: with_halo(): after = lax.ppermute(leading, axis, down)]
    pallas_call x0 -> x1, Pallas kernels: none -> 66.5 us  [shards(): pl.pallas_call(functools.partial(kernel, cfg), out_shape=(jax.ShapeDtypeS...]
    dot_general x19 -> x0, matrix products: 59.5 us -> none  [the longest x18 58.6 us: forcing(): jnp.einsum('gro,oc->grc', weighted_rows, col_hit, precision=lax.Precision...]
    psum x4 -> x0, blocking collectives: 49.2 us -> none  [one_axis_at_a_time(): value = lax.psum(value, axis)]
    while x306 -> x0, local copies, waits for them, and re-layouts: 30.8 us -> none
    slice x58 -> x0, local copies, waits for them, and re-layouts: 24.2 us -> none  [the longest x9 12.3 us: forcing(): local_row[step][None, :] == row_range[:, None]]
    concatenate x37 -> x0, other arithmetic: 16.9 us -> none  [the longest x19 10.1 us: with_halo(): value = jnp.concatenate([before, value, after], axis=dim)]
  transfers between devices with their start and end apart: 49 -> 0, of which waited for: 28 -> 0; matrix products, arithmetic and copies ran while one was open for 2% -> 0% of each run, Pallas kernels for 0% -> 0%
where the time goes in v1:
time: 76.6 us; the launch traced here: 76.2 us
  Pallas kernels  66.5 us (87%)
  local copies, waits for them, and re-layouts  9 us (12%)
    pallas_call x1, Pallas kernels, shards(): pl.pallas_call(functools.partial(kernel, cfg), out_shape=(jax.ShapeDtypeS...  66.5 us
    unnamed x19, local copies, waits for them, and re-layouts  9 us

profile of v1, /device:TPU:1, one launch (start us, length us, event | category | flops | bytes accessed | tf_op | source)
XLA Modules:
  0.0 76.2 jit_solution(4665741049936027222)
XLA Ops:
  0.6 0.0 copy-start
  0.6 1.1 %copy-done = f32[1,3,16,4096]{3,2,1,0:T(8,128)S(1)} copy-done((f32[1,3,16,4096]{3,2,1,0:T(8,128)S(1)}, f32[1,3,16,4096]{3,2,1,0:T(8,128)}, u32[]{:S(2)}) %copy-start) | copy-done | bytes 786456
  1.8 0.0 copy-start.1
  1.8 1.0 %copy-done.1 = f32[2,16,4096]{2,1,0:T(8,128)S(1)} copy-done((f32[2,16,4096]{2,1,0:T(8,128)S(1)}, f32[2,16,4096]{2,1,0:T(8,128)}, u32[]{:S(2)}) %copy-start.1) | copy-done | bytes 524312
  2.8 0.0 copy-start.2
  2.8 0.9 %copy-done.2 = f32[16,4096]{1,0:T(8,128)S(1)} copy-done((f32[16,4096]{1,0:T(8,128)S(1)}, f32[16,4096]{1,0:T(8,128)}, u32[]{:S(2)}) %copy-start.2) | copy-done | bytes 262168
  3.8 0.0 copy-start.3
  3.8 0.9 %copy-done.3 = f32[16,4096]{1,0:T(8,128)S(1)} copy-done((f32[16,4096]{1,0:T(8,128)S(1)}, f32[16,4096]{1,0:T(8,128)}, u32[]{:S(2)}) %copy-start.3) | copy-done | bytes 262168
  4.7 0.0 copy-start.4
  4.7 0.9 %copy-done.4 = f32[16,4096]{1,0:T(8,128)S(1)} copy-done((f32[16,4096]{1,0:T(8,128)S(1)}, f32[16,4096]{1,0:T(8,128)}, u32[]{:S(2)}) %copy-start.4) | copy-done | bytes 262168
  5.7 0.0 copy-start.5
  5.7 0.7 copy-done.5
  6.4 0.0 copy-start.6
  6.4 0.7 copy-done.6
  7.0 0.0 copy-start.7
  7.0 0.7 copy-done.7
  7.7 66.5 %shard_map.103 = (f32[1,2,16,4096]{3,2,1,0:T(8,128)S(1)}, f32[16,512]{1,0:T(8,128)S(1)}, f32[2]{0:T(128)S(1)}) custom-call(f32[1,3,16,4096]{3,2,1,0:T(8,128)S(1)} %copy-done, f32[16,4096]{1,0:T(8,128)S(1)} %copy-done.2, f32[16,4096]{1,0:T(8,128)S(1)} %copy-done.3, f32[16,4096]{1,0:T(8,128)S(1)} %copy-done.4, f32[2,16,4096]{2,1,0:T(8,128)S(1)} %copy-done.1, ...), custom_call_target="tpu_custom_call" | custom-call | tf_op jit(solution)/shard_map/pallas_call | solution.py:362
  74.3 0.8 %copy.14 = f32[1,2,16,4096]{3,2,1,0:T(8,128)} copy(f32[1,2,16,4096]{3,2,1,0:T(8,128)S(1)} %get-tuple-element.6) | data formatting | bytes 1048576
  75.1 0.6 copy.15
  75.7 0.5 copy.16
Async XLA Ops:
  0.6 1.1 %copy-start = (f32[1,3,16,4096]{3,2,1,0:T(8,128)S(1)}, f32[1,3,16,4096]{3,2,1,0:T(8,128)}, u32[]{:S(2)}) copy-start(f32[1,3,16,4096]{3,2,1,0:T(8,128)} %heads.1) | copy-start | bytes 2359300
  1.8 1.0 %copy-start.1 = (f32[2,16,4096]{2,1,0:T(8,128)S(1)}, f32[2,16,4096]{2,1,0:T(8,128)}, u32[]{:S(2)}) copy-start(f32[2,16,4096]{2,1,0:T(8,128)} %term.1) | copy-start | bytes 1572868
  2.8 0.9 %copy-start.2 = (f32[16,4096]{1,0:T(8,128)S(1)}, f32[16,4096]{1,0:T(8,128)}, u32[]{:S(2)}) copy-start(f32[16,4096]{1,0:T(8,128)} %cap.1) | copy-start | bytes 786436
  3.8 0.9 %copy-start.3 = (f32[16,4096]{1,0:T(8,128)S(1)}, f32[16,4096]{1,0:T(8,128)}, u32[]{:S(2)}) copy-start(f32[16,4096]{1,0:T(8,128)} %crow.1) | copy-start | bytes 786436
  4.7 0.9 %copy-start.4 = (f32[16,4096]{1,0:T(8,128)S(1)}, f32[16,4096]{1,0:T(8,128)}, u32[]{:S(2)}) copy-start(f32[16,4096]{1,0:T(8,128)} %ccol.1) | copy-start | bytes 786436
  5.7 0.7 copy-start.5
  6.4 0.7 copy-start.6
  7.0 0.7 copy-start.7

commit v2 on v1

--- a/solution.py
+++ b/solution.py
@@ -153,7 +153,8 @@
                     + got[begin + 2 * tall : begin + 3 * tall])
         return carry
 
-    lax.fori_loop(0, planes, forcing, 0)
+    half = planes // 2
+    lax.fori_loop(half, planes, forcing, 0)
 
     for copy in halos:
         copy.wait_recv()
@@ -214,7 +215,7 @@
                  + coef[2, strip, :][None] * down + coef[3, strip, :][None] * up)
         return here, total, strip
 
-    def one_step(now, section, step):
+    def one_step(now, section, step, skip):
         def first_sweep(i, carry):
             here, total, strip = stencil(now, i)
             part = (coef[4, strip, :][None] * here
@@ -228,8 +229,8 @@
             now[:, strip, :] = rhs[:, strip, :] + total
             return carry
 
-        lax.fori_loop(0, strips, first_sweep, 0)
-        lax.fori_loop(0, strips, second_sweep, 0)
+        lax.fori_loop(skip, strips - skip, first_sweep, 0)
+        lax.fori_loop(skip, strips - skip, second_sweep, 0)
         saved[section, step] = now[:, rows : 2 * rows, LANES:]
 
     def start_copy(section, d):
@@ -243,15 +244,15 @@
             out_a.at[0, :, :, pl.ds(pl.multiple_of(first, LANES), cols)],
             loc_sem.at[0])
 
-    half = planes // 2
     mids = []
     for phase in range(2):
         now = field.at[phase]
 
         def one_section(turn, carry):
             section = planes - 1 - phase * half - turn
+            skip = turn * 2 * STEPS // 8
             for step in reversed(range(STEPS)):
-                one_step(now, section, step)
+                one_step(now, section, step, skip)
             d = lax.rem(section - me + planes, planes)
 
             @pl.when(section != me)
@@ -273,15 +274,21 @@
                               mid_send.at[way], mid_recv.at[way], me, target)
                 copy.start()
                 mids.append(copy)
+            lax.fori_loop(0, half, forcing, 0)
             for copy in mids:
                 copy.wait_recv()
 
-    for d in range(1, planes):
-        for copy in head_copies(d, plane_at(planes - d)):
-            copy.wait_recv()
-
-    def sums(section, carry):
+
+    def sums(turn, carry):
         sens, store_0, store_1 = carry
+        d = jnp.where(turn % 2 == 1, (turn + 1) // 2, lax.rem(planes - turn // 2, planes))
+        section = plane_at(planes - d)
+
+        @pl.when(turn > 0)
+        def _():
+            for copy in head_copies(d, section):
+                copy.wait_recv()
+
         for step in range(STEPS):
             a_0 = saved[section, step, 0]
             a_1 = saved[section, step, 1]
@@ -398,7 +405,7 @@
                 dma((planes + inner + outer,)),
             ],
             compiler_params=pltpu.CompilerParams(
-                collective_id=0, has_side_effects=True, vmem_limit_bytes=48 * 1024 * 1024
+                collective_id=0, has_side_effects=True, vmem_limit_bytes=67043328
             ),
         )(heads, capacity, cond_row, cond_col, terminal, obs_cell, obs_weight, block_mask)
         return out

time: 76.6 us -> 65.1 us (0.85)
  local copies, waits for them, and re-layouts: 9 us -> 3.05 us
  Pallas kernels: 66.5 us -> 61.2 us
    unnamed x19 -> x7, local copies, waits for them, and re-layouts: 9 us -> 3.05 us
    pallas_call x1, Pallas kernels: 66.5 us -> 61.2 us  [shards(): pl.pallas_call(functools.partial(kernel, cfg), out_shape=(jax.ShapeDtypeS...]
where the time goes in v2:
time: 65.1 us; the launch traced here: 64.9 us
  Pallas kernels  61.2 us (94%)
  local copies, waits for them, and re-layouts  3.05 us (5%)
    pallas_call x1, Pallas kernels, shards(): pl.pallas_call(functools.partial(kernel, cfg), out_shape=(jax.ShapeDtypeS...  61.2 us
    unnamed x7, local copies, waits for them, and re-layouts  3.05 us

profile of v2, /device:TPU:1, one launch (start us, length us, event | category | flops | bytes accessed | tf_op | source)
XLA Modules:
  0.0 64.9 jit_solution(12595088641637277631)
XLA Ops:
  0.6 61.2 %shard_map.103 = (f32[1,2,16,4096]{3,2,1,0:T(8,128)}, f32[16,512]{1,0:T(8,128)}, f32[2]{0:T(128)}) custom-call(f32[1,3,16,4096]{3,2,1,0:T(8,128)} %heads.1, f32[16,4096]{1,0:T(8,128)} %cap.1, f32[16,4096]{1,0:T(8,128)} %crow.1, f32[16,4096]{1,0:T(8,128)} %ccol.1, f32[2,16,4096]{2,1,0:T(8,128)} %term.1, s32[1,2,512]{2,1,0:T(2,128)} %ocell.1, ...), custom_call_target="tpu_custom_call" | custom-call | tf_op jit(solution)/shard_map/pallas_call | solution.py:369
  61.9 0.0 copy-start
  61.9 1.9 %copy.14 = f32[1,2,16,4096]{3,2,1,0:T(8,128)} copy(f32[1,2,16,4096]{3,2,1,0:T(8,128)} %get-tuple-element.6) | data formatting | bytes 1048576
  63.8 0.0 copy-done
  63.8 0.0 copy-start.1
  63.8 0.6 copy.15
  64.4 0.0 copy-done.1
  64.4 0.5 copy.16
Async XLA Ops:
  61.9 1.9 %copy-start = (f32[16,512]{1,0:T(8,128)S(1)}, f32[16,512]{1,0:T(8,128)}, u32[]{:S(2)}) copy-start(f32[16,512]{1,0:T(8,128)} %get-tuple-element.7) | copy-start | bytes 98308
  63.8 0.7 %copy-start.1 = (f32[2]{0:T(128)S(1)}, f32[2]{0:T(128)}, u32[]{:S(2)}) copy-start(f32[2]{0:T(128)} %get-tuple-element.8) | copy-start | bytes 28

commit v3 on v2

--- a/solution.py
+++ b/solution.py
@@ -13,10 +13,10 @@
 
 
 def kernel(cfg, heads, cap, crow, ccol, term, ocell, oweight, mask, out_a, out_c, out_s,
-           ext, field, mid, rhs, coef, force, cells, weights, head, saved, red_a, red_b, red_c,
+           ext, field, mid, rhs, coef, force, cells, weights, head, saved, red_a, red_b,
            loc_sem, halo_send, halo_recv, obs_send, obs_recv, head_send, head_recv,
            mid_send, mid_recv, start_send, start_recv, red_send, red_recv):
-    planes, tiles, inner, rows, cols, total_cols, block_rows, block_cols = cfg
+    planes, tiles, rows, cols, total_cols, block_rows, block_cols = cfg
     wide = cols + 2 * LANES
     tall = 3 * rows
     edge = cols + LANES
@@ -25,26 +25,18 @@
     tile = lax.axis_index("tile")
     above = lax.rem(tile + tiles - 1, tiles)
     below = lax.rem(tile + 1, tiles)
-    group = tile // inner
-    place = lax.rem(tile, inner)
-    outer = tiles // inner
 
     def plane_at(d):
         return lax.rem(me + d, planes)
 
-    def inner_at(d):
-        return group * inner + lax.rem(place + d, inner)
-
-    def outer_at(d):
-        return lax.rem(group + d, outer) * inner + place
+    def tile_at(d):
+        return lax.rem(tile + d, tiles)
 
     def at(plane, row_tile):
         return {"tm": plane, "tile": row_tile}
 
     partners = [(plane_at(d), tile) for d in range(1, planes)]
-    partners += [(me, above), (me, below)]
-    partners += [(me, inner_at(d)) for d in range(1, inner)]
-    partners += [(me, outer_at(d)) for d in range(1, outer)]
+    partners += [(me, tile_at(d)) for d in range(1, tiles)]
     barrier = pltpu.get_barrier_semaphore()
     for plane, row_tile in partners:
         pl.semaphore_signal(barrier, inc=1, device_id=at(plane, row_tile), device_id_type=MESH)
@@ -229,8 +221,8 @@
             now[:, strip, :] = rhs[:, strip, :] + total
             return carry
 
-        lax.fori_loop(skip, strips - skip, first_sweep, 0)
-        lax.fori_loop(skip, strips - skip, second_sweep, 0)
+        lax.fori_loop(skip, strips - skip, first_sweep, 0, unroll=True)
+        lax.fori_loop(skip, strips - skip, second_sweep, 0, unroll=True)
         saved[section, step] = now[:, rows : 2 * rows, LANES:]
 
     def start_copy(section, d):
@@ -248,9 +240,8 @@
     for phase in range(2):
         now = field.at[phase]
 
-        def one_section(turn, carry):
+        def one_section(skip, turn, carry):
             section = planes - 1 - phase * half - turn
-            skip = turn * 2 * STEPS // 8
             for step in reversed(range(STEPS)):
                 one_step(now, section, step, skip)
             d = lax.rem(section - me + planes, planes)
@@ -265,7 +256,8 @@
 
             return carry
 
-        lax.fori_loop(0, half, one_section, 0)
+        lax.fori_loop(0, half // 2, functools.partial(one_section, 0), 0)
+        lax.fori_loop(half // 2, half, functools.partial(one_section, 1), 0)
         if phase == 0:
             core = pl.ds(rows, rows)
             field[1, :, rows : 2 * rows, :] = field[0, :, rows : 2 * rows, :]
@@ -306,7 +298,7 @@
     sens, store_0, store_1 = lax.fori_loop(0, planes, sums, (zero, zero, zero))
     out_c[...] = sens * pair_core
     cap_core = ext[0, rows : 2 * rows, LANES : LANES + cols]
-    tile_lane = lax.broadcasted_iota(jnp.int32, (8, LANES), 1)
+    tile_lane = lax.broadcasted_iota(jnp.int32, (1, LANES), 1)
     part = jnp.where(tile_lane == 0, jnp.sum(store_0 * cap_core), 0.0)
     part = jnp.where(tile_lane == 1, jnp.sum(store_1 * cap_core), part)
 
@@ -327,16 +319,12 @@
             remote(slots.at[source], slots.at[source], red_send.at[base + d],
                    red_recv.at[base + d], plane, row_tile).wait_recv()
         reduce_sends.extend(copies)
-        total = slots[0]
-        for i in range(1, count):
-            total = total + slots[i]
-        return total
-
-    part = exchange(part, red_b, place, inner, lambda d: (me, inner_at(d)), 0)
-    part = exchange(part, red_c, group, outer, lambda d: (me, outer_at(d)), inner)
-    part = exchange(part, red_a, me, planes, lambda d: (plane_at(d), tile), inner + outer)
-    out_s[0] = jnp.sum(jnp.where(tile_lane[:1] == 0, part[:1], 0.0))
-    out_s[1] = jnp.sum(jnp.where(tile_lane[:1] == 1, part[:1], 0.0))
+        return jnp.sum(slots[...], axis=0)
+
+    part = exchange(part, red_b, tile, tiles, lambda d: (me, tile_at(d)), 0)
+    part = exchange(part, red_a, me, planes, lambda d: (plane_at(d), tile), tiles)
+    out_s[0] = jnp.sum(jnp.where(tile_lane == 0, part, 0.0))
+    out_s[1] = jnp.sum(jnp.where(tile_lane == 1, part, 0.0))
 
     own_start().wait()
     for d in range(1, planes):
@@ -352,8 +340,6 @@
 
 def solution(mesh):
     planes, tiles = mesh.shape["tm"], mesh.shape["tile"]
-    inner = min(8, tiles // 2)
-    outer = tiles // inner
 
     def shards(heads, capacity, cond_row, cond_col, terminal, obs_cell, obs_weight, block_mask):
         rows, total_cols = capacity.shape
@@ -362,7 +348,7 @@
         observed = obs_cell.shape[2]
         block_rows = rows * tiles // block_mask.shape[0]
         block_cols = total_cols // block_mask.shape[1]
-        cfg = (planes, tiles, inner, rows, cols, total_cols, block_rows, block_cols)
+        cfg = (planes, tiles, rows, cols, total_cols, block_rows, block_cols)
         f32 = jnp.float32
         dma = pltpu.SemaphoreType.DMA
         any_spec = pl.BlockSpec(memory_space=pl.ANY)
@@ -387,9 +373,8 @@
                 pltpu.VMEM((planes, STEPS, 2, observed), f32),
                 pltpu.VMEM((planes, 3, rows, edge), f32),
                 pltpu.VMEM((planes, STEPS, 2, rows, edge), f32),
-                pltpu.VMEM((planes, 8, LANES), f32),
-                pltpu.VMEM((inner, 8, LANES), f32),
-                pltpu.VMEM((outer, 8, LANES), f32),
+                pltpu.VMEM((planes, 1, LANES), f32),
+                pltpu.VMEM((tiles, 1, LANES), f32),
                 dma((16,)),
                 dma((2, 12)),
                 dma((2, 12)),
@@ -401,8 +386,8 @@
                 dma((2,)),
                 dma((planes,)),
                 dma((planes,)),
-                dma((planes + inner + outer,)),
-                dma((planes + inner + outer,)),
+                dma((planes + tiles,)),
+                dma((planes + tiles,)),
             ],
             compiler_params=pltpu.CompilerParams(
                 collective_id=0, has_side_effects=True, vmem_limit_bytes=67043328

time: 65.1 us -> 56 us (0.86)
  Pallas kernels: 61.2 us -> 52.2 us
    pallas_call x1, Pallas kernels: 61.2 us -> 52.2 us  [shards(): pl.pallas_call(functools.partial(kernel, cfg), out_shape=(jax.ShapeDtypeS...]
where the time goes in v3:
time: 56 us; the launch traced here: 55.9 us
  Pallas kernels  52.2 us (93%)
  local copies, waits for them, and re-layouts  3.05 us (5%)
  between operations  0.65 us (1%)
    pallas_call x1, Pallas kernels, shards(): pl.pallas_call(functools.partial(kernel, cfg), out_shape=(jax.ShapeDtypeS...  52.2 us
    unnamed x7, local copies, waits for them, and re-layouts  3.05 us

profile of v3, /device:TPU:1, one launch (start us, length us, event | category | flops | bytes accessed | tf_op | source)
XLA Modules:
  0.0 55.9 jit_solution(2147746093105568204)
XLA Ops:
  0.6 52.2 %shard_map.103 = (f32[1,2,16,4096]{3,2,1,0:T(8,128)}, f32[16,512]{1,0:T(8,128)}, f32[2]{0:T(128)}) custom-call(f32[1,3,16,4096]{3,2,1,0:T(8,128)} %heads.1, f32[16,4096]{1,0:T(8,128)} %cap.1, f32[16,4096]{1,0:T(8,128)} %crow.1, f32[16,4096]{1,0:T(8,128)} %ccol.1, f32[2,16,4096]{2,1,0:T(8,128)} %term.1, s32[1,2,512]{2,1,0:T(2,128)} %ocell.1, ...), custom_call_target="tpu_custom_call" | custom-call | tf_op jit(solution)/shard_map/pallas_call | solution.py:355
  52.8 0.0 copy-start
  52.8 1.9 %copy.14 = f32[1,2,16,4096]{3,2,1,0:T(8,128)} copy(f32[1,2,16,4096]{3,2,1,0:T(8,128)} %get-tuple-element.6) | data formatting | bytes 1048576
  54.7 0.0 copy-done
  54.7 0.0 copy-start.1
  54.7 0.6 %copy.15 = f32[16,512]{1,0:T(8,128)} copy(f32[16,512]{1,0:T(8,128)S(1)} %copy-done) | data formatting | bytes 65536
  55.3 0.0 copy-done.1
  55.4 0.5 copy.16
Async XLA Ops:
  52.8 1.9 %copy-start = (f32[16,512]{1,0:T(8,128)S(1)}, f32[16,512]{1,0:T(8,128)}, u32[]{:S(2)}) copy-start(f32[16,512]{1,0:T(8,128)} %get-tuple-element.7) | copy-start | bytes 98308
  54.7 0.7 %copy-start.1 = (f32[2]{0:T(128)S(1)}, f32[2]{0:T(128)}, u32[]{:S(2)}) copy-start(f32[2]{0:T(128)} %get-tuple-element.8) | copy-start | bytes 28

commit v4 on v3

--- a/solution.py
+++ b/solution.py
@@ -13,9 +13,10 @@
 
 
 def kernel(cfg, heads, cap, crow, ccol, term, ocell, oweight, mask, out_a, out_c, out_s,
-           ext, field, mid, rhs, coef, force, cells, weights, head, saved, red_a, red_b,
+           ext, field, mid, rhs, coef, force, cells, weights, head, saved, red_a, red_b, edge_out, edge_in,
            loc_sem, halo_send, halo_recv, obs_send, obs_recv, head_send, head_recv,
-           mid_send, mid_recv, start_send, start_recv, red_send, red_recv):
+           mid_send, mid_recv, start_send, start_recv, red_send, red_recv,
+           edge_send, edge_recv):
     planes, tiles, rows, cols, total_cols, block_rows, block_cols = cfg
     wide = cols + 2 * LANES
     tall = 3 * rows
@@ -63,12 +64,7 @@
 
     def head_parts(target, source):
         begin = lane(target * cols)
-        after = lane(target * cols + cols)
-        return [
-            (heads.at[0, :, :, pl.ds(begin, cols)], head.at[source, :, :, pl.ds(0, cols)]),
-            (heads.at[0, pl.ds(1, 2), :, pl.ds(after, LANES)],
-             head.at[source, pl.ds(1, 2), :, pl.ds(cols, LANES)]),
-        ]
+        return [(heads.at[0, :, :, pl.ds(begin, cols)], head.at[source])]
 
     def obs_parts(source):
         return [(ocell.at[0], cells.at[source]), (oweight.at[0], weights.at[source])]
@@ -272,7 +268,7 @@
 
 
     def sums(turn, carry):
-        sens, store_0, store_1 = carry
+        sens, store_0, store_1, jumps, begins, ends = carry
         d = jnp.where(turn % 2 == 1, (turn + 1) // 2, lax.rem(planes - turn // 2, planes))
         section = plane_at(planes - d)
 
@@ -286,17 +282,24 @@
             a_1 = saved[section, step, 1]
             later = head[section, step + 1]
             both = a_0 + a_1
-            jump = ((pltpu.roll(both, edge - 1, 1) - both)
-                    * (pltpu.roll(later, edge - 1, 1) - later))
-            sens = sens + jump[:, :cols]
-            change = later[:, :cols] - head[section, step, :, pl.ds(0, cols)]
+            jump = pltpu.roll(both, edge - 1, 1) - both
+            sens = sens + jump[:, :cols] * (pltpu.roll(later, cols - 1, 1) - later)
+            here = lane_id == section * STEPS + step
+            jumps = jnp.where(here, jump[:, cols - 1 : cols], jumps)
+            begins = jnp.where(here, later[:, 0:1], begins)
+            ends = jnp.where(here, later[:, cols - 1 : cols], ends)
+            change = later - head[section, step]
             store_0 = store_0 + a_0[:, :cols] * change
             store_1 = store_1 + a_1[:, :cols] * change
-        return sens, store_0, store_1
+        return sens, store_0, store_1, jumps, begins, ends
 
     zero = jnp.zeros((rows, cols), jnp.float32)
-    sens, store_0, store_1 = lax.fori_loop(0, planes, sums, (zero, zero, zero))
-    out_c[...] = sens * pair_core
+    none = jnp.zeros((rows, LANES), jnp.float32)
+    sens, store_0, store_1, jumps, begins, ends = lax.fori_loop(
+        0, planes, sums, (zero, zero, zero, none, none, none))
+    edge_out[...] = begins
+    edge_copy = remote(edge_out, edge_in, edge_send, edge_recv, plane_at(planes - 1), tile)
+    edge_copy.start()
     cap_core = ext[0, rows : 2 * rows, LANES : LANES + cols]
     tile_lane = lax.broadcasted_iota(jnp.int32, (1, LANES), 1)
     part = jnp.where(tile_lane == 0, jnp.sum(store_0 * cap_core), 0.0)
@@ -326,6 +329,11 @@
     out_s[0] = jnp.sum(jnp.where(tile_lane == 0, part, 0.0))
     out_s[1] = jnp.sum(jnp.where(tile_lane == 1, part, 0.0))
 
+    edge_copy.wait_recv()
+    last = jnp.sum(jumps * (edge_in[...] - ends), axis=1, keepdims=True)
+    col = lax.broadcasted_iota(jnp.int32, (rows, cols), 1)
+    out_c[...] = jnp.where(col == cols - 1, last, sens) * pair_core
+
     own_start().wait()
     for d in range(1, planes):
         source = plane_at(planes - d)
@@ -334,7 +342,7 @@
                start_send.at[d], start_recv.at[d], plane_at(d), tile).wait_recv()
     for d in range(1, planes):
         start_copy(plane_at(d), d).wait_send()
-    for copy in sent + halos + sent_heads + mids + reduce_sends:
+    for copy in sent + halos + sent_heads + mids + reduce_sends + [edge_copy]:
         copy.wait_send()
 
 
@@ -371,10 +379,12 @@
                 pltpu.VMEM((planes, STEPS, 2, tall, wide), f32),
                 pltpu.VMEM((planes, STEPS, observed), jnp.int32),
                 pltpu.VMEM((planes, STEPS, 2, observed), f32),
-                pltpu.VMEM((planes, 3, rows, edge), f32),
+                pltpu.VMEM((planes, 3, rows, cols), f32),
                 pltpu.VMEM((planes, STEPS, 2, rows, edge), f32),
                 pltpu.VMEM((planes, 1, LANES), f32),
                 pltpu.VMEM((tiles, 1, LANES), f32),
+                pltpu.VMEM((rows, LANES), f32),
+                pltpu.VMEM((rows, LANES), f32),
                 dma((16,)),
                 dma((2, 12)),
                 dma((2, 12)),
@@ -388,6 +398,8 @@
                 dma((planes,)),
                 dma((planes + tiles,)),
                 dma((planes + tiles,)),
+                dma(()),
+                dma(()),
             ],
             compiler_params=pltpu.CompilerParams(
                 collective_id=0, has_side_effects=True, vmem_limit_bytes=67043328

time: 56 us -> 53.7 us (0.959)
  Pallas kernels: 52.2 us -> 49.9 us
    pallas_call x1, Pallas kernels: 52.2 us -> 49.9 us  [shards(): pl.pallas_call(functools.partial(kernel, cfg), out_shape=(jax.ShapeDtypeS...]
where the time goes in v4:
time: 53.7 us; the launch traced here: 53.6 us
  Pallas kernels  49.9 us (93%)
  local copies, waits for them, and re-layouts  3.05 us (6%)
  between operations  0.65 us (1%)
    pallas_call x1, Pallas kernels, shards(): pl.pallas_call(functools.partial(kernel, cfg), out_shape=(jax.ShapeDtypeS...  49.9 us
    unnamed x7, local copies, waits for them, and re-layouts  3.05 us

profile of v4, /device:TPU:1, one launch (start us, length us, event | category | flops | bytes accessed | tf_op | source)
XLA Modules:
  0.0 53.6 jit_solution(15974500835065230835)
XLA Ops:
  0.6 49.9 %shard_map.103 = (f32[1,2,16,4096]{3,2,1,0:T(8,128)}, f32[16,512]{1,0:T(8,128)}, f32[2]{0:T(128)}) custom-call(f32[1,3,16,4096]{3,2,1,0:T(8,128)} %heads.1, f32[16,4096]{1,0:T(8,128)} %cap.1, f32[16,4096]{1,0:T(8,128)} %crow.1, f32[16,4096]{1,0:T(8,128)} %ccol.1, f32[2,16,4096]{2,1,0:T(8,128)} %term.1, s32[1,2,512]{2,1,0:T(2,128)} %ocell.1, ...), custom_call_target="tpu_custom_call" | custom-call | tf_op jit(solution)/shard_map/pallas_call | solution.py:363
  50.5 0.0 copy-start
  50.5 1.9 %copy.14 = f32[1,2,16,4096]{3,2,1,0:T(8,128)} copy(f32[1,2,16,4096]{3,2,1,0:T(8,128)} %get-tuple-element.6) | data formatting | bytes 1048576
  52.4 0.0 copy-done
  52.4 0.0 copy-start.1
  52.4 0.6 %copy.15 = f32[16,512]{1,0:T(8,128)} copy(f32[16,512]{1,0:T(8,128)S(1)} %copy-done) | data formatting | bytes 65536
  53.0 0.0 copy-done.1
  53.0 0.5 copy.16
Async XLA Ops:
  50.5 1.9 %copy-start = (f32[16,512]{1,0:T(8,128)S(1)}, f32[16,512]{1,0:T(8,128)}, u32[]{:S(2)}) copy-start(f32[16,512]{1,0:T(8,128)} %get-tuple-element.7) | copy-start | bytes 98308
  52.4 0.7 %copy-start.1 = (f32[2]{0:T(128)S(1)}, f32[2]{0:T(128)}, u32[]{:S(2)}) copy-start(f32[2]{0:T(128)} %get-tuple-element.8) | copy-start | bytes 28

commit v5 on v4

--- a/solution.py
+++ b/solution.py
@@ -97,7 +97,7 @@
         for i, (src, dst) in enumerate(own_parts(row)):
             halos.append(remote(src, dst, halo_send.at[way, i], halo_recv.at[way, i], me, target))
     order = sorted(range(1, planes), key=lambda d: -min(d, planes - d))
-    for copy in sent + halos:
+    for copy in halos + sent:
         copy.start()
     sent_heads = []
     for d in order:
@@ -142,7 +142,7 @@
         return carry
 
     half = planes // 2
-    lax.fori_loop(half, planes, forcing, 0)
+    lax.fori_loop(half, planes, forcing, 0, unroll=2)
 
     for copy in halos:
         copy.wait_recv()
@@ -252,8 +252,8 @@
 
             return carry
 
-        lax.fori_loop(0, half // 2, functools.partial(one_section, 0), 0)
-        lax.fori_loop(half // 2, half, functools.partial(one_section, 1), 0)
+        lax.fori_loop(0, half // 2, functools.partial(one_section, 0), 0, unroll=True)
+        lax.fori_loop(half // 2, half, functools.partial(one_section, 1), 0, unroll=True)
         if phase == 0:
             core = pl.ds(rows, rows)
             field[1, :, rows : 2 * rows, :] = field[0, :, rows : 2 * rows, :]

time: 53.7 us -> 53.6 us (level)
  no operation moved by 1% of the time
where the time goes in v5:
time: 53.6 us; the launch traced here: 53.4 us
  Pallas kernels  49.7 us (93%)
  local copies, waits for them, and re-layouts  3.05 us (6%)
  between operations  0.65 us (1%)
    pallas_call x1, Pallas kernels, shards(): pl.pallas_call(functools.partial(kernel, cfg), out_shape=(jax.ShapeDtypeS...  49.7 us
    unnamed x7, local copies, waits for them, and re-layouts  3.05 us

profile of v5, /device:TPU:1, one launch (start us, length us, event | category | flops | bytes accessed | tf_op | source)
XLA Modules:
  0.0 53.4 jit_solution(5504054385951998282)
XLA Ops:
  0.6 49.7 %shard_map.103 = (f32[1,2,16,4096]{3,2,1,0:T(8,128)}, f32[16,512]{1,0:T(8,128)}, f32[2]{0:T(128)}) custom-call(f32[1,3,16,4096]{3,2,1,0:T(8,128)} %heads.1, f32[16,4096]{1,0:T(8,128)} %cap.1, f32[16,4096]{1,0:T(8,128)} %crow.1, f32[16,4096]{1,0:T(8,128)} %ccol.1, f32[2,16,4096]{2,1,0:T(8,128)} %term.1, s32[1,2,512]{2,1,0:T(2,128)} %ocell.1, ...), custom_call_target="tpu_custom_call" | custom-call | tf_op jit(solution)/shard_map/pallas_call | solution.py:363
  50.4 0.0 copy-start
  50.4 1.9 %copy.14 = f32[1,2,16,4096]{3,2,1,0:T(8,128)} copy(f32[1,2,16,4096]{3,2,1,0:T(8,128)} %get-tuple-element.6) | data formatting | bytes 1048576
  52.2 0.0 copy-done
  52.2 0.0 copy-start.1
  52.2 0.6 %copy.15 = f32[16,512]{1,0:T(8,128)} copy(f32[16,512]{1,0:T(8,128)S(1)} %copy-done) | data formatting | bytes 65536
  52.9 0.0 copy-done.1
  52.9 0.5 copy.16
Async XLA Ops:
  50.4 1.9 %copy-start = (f32[16,512]{1,0:T(8,128)S(1)}, f32[16,512]{1,0:T(8,128)}, u32[]{:S(2)}) copy-start(f32[16,512]{1,0:T(8,128)} %get-tuple-element.7) | copy-start | bytes 98308
  52.2 0.7 %copy-start.1 = (f32[2]{0:T(128)S(1)}, f32[2]{0:T(128)}, u32[]{:S(2)}) copy-start(f32[2]{0:T(128)} %get-tuple-element.8) | copy-start | bytes 28
